TPU v7x, 32 devices: a whole 2x2x4 slice. The times are simulated.
32 devices in a mesh: gx: 4 (over y, core), gy: 2 (over x), gz: 4 (over z).
Axes of the slice: x: 2, y: 2, z: 4, core: 2. Of those that a mesh axis runs over, the one named last changes fastest.
Arguments:
- adjoint: float32 [64, 32, 512], P('gx', 'gy', 'gz'), may hold values from -6 to 6
- element_zone_index: int32 [16, 8, 128], P('gx', 'gy', 'gz'), may hold values from 0 to 7
- kappa_table: float32 [8], replicated, may hold values from 2 to 8
Outputs:
- prior_grad: float32 [64, 32, 512], P('gx', 'gy', 'gz')
- kappa_grad: float32 [16, 8, 128], P('gx', 'gy', 'gz')
All inputs are finite; a program needn't handle non-finite values.
Results may differ from a plain program's by a relative error of at most 0.0001.
Values sent between devices are 32-bit elements; how exact they have to be, the bound alone decides.
A program may use at most 64 MiB of HBM per device.

v0:
```python
import functools
import itertools
import math

import jax
import jax.numpy as jnp
import numpy as np
from jax import lax
from jax.experimental import pallas as pl
from jax.experimental.pallas import tpu as pltpu
from jax.sharding import PartitionSpec as P

AXES = ("gx", "gy", "gz")
HIGHEST = lax.Precision.HIGHEST
OFFSETS = [o for o in itertools.product((0, 1), repeat=3) if sum(o) > 0]


def gll_tables():
    points = np.array([-1.0, -math.sqrt(3.0 / 7.0), 0.0, math.sqrt(3.0 / 7.0), 1.0])
    weights = np.array([0.1, 49.0 / 90.0, 32.0 / 45.0, 49.0 / 90.0, 0.1])
    scales = np.array(
        [np.prod([points[r] - points[o] for o in range(5) if o != r]) for r in range(5)]
    )
    derivative = np.zeros((5, 5))
    for r in range(5):
        for c in range(5):
            if r != c:
                derivative[r, c] = scales[r] / scales[c] / (points[r] - points[c])
        derivative[r, r] = -np.sum(derivative[r])
    return weights, derivative.T @ (weights[:, None] * derivative)


WEIGHTS, STIFF = gll_tables()
LUMPED = np.array([2 * WEIGHTS[0], WEIGHTS[1], WEIGHTS[2], WEIGHTS[3]])
WN = WEIGHTS[:4] / LUMPED
WN0 = float(WEIGHTS[4] / LUMPED[0])
END_DIAG = float(STIFF[4, 4] / LUMPED[0])


def constants(ez):
    nodes = 4 * ez
    stiff_z = np.zeros((nodes, nodes))
    zexp = np.zeros((ez, 2 * nodes))
    zred = np.zeros((2, nodes, ez))
    for e in range(ez):
        for a in range(5):
            k = 4 * e + a
            if k < nodes:
                zexp[e, k] += WEIGHTS[a] / LUMPED[a % 4]
                zred[0, k, e] += WEIGHTS[a]
                for b in range(5):
                    if 4 * e + b < nodes:
                        stiff_z[4 * e + b, k] += STIFF[a, b] / LUMPED[a % 4]
    zexp[ez - 1, nodes] = WN0
    zred[1, 0, ez - 1] = WEIGHTS[4]
    return tuple(np.asarray(c, np.float32) for c in (stiff_z, zexp, zred))


def dot(a, b):
    return jnp.dot(a, b, precision=HIGHEST, preferred_element_type=jnp.float32)


def weighted(layers, coef):
    total = None
    for n, c in sorted(coef.items()):
        term = layers[n] * jnp.float32(c)
        total = term if total is None else total + term
    return total


def line_terms(layers, elems):
    out = []
    for i in range(4 * elems):
        e, a = divmod(i, 4)
        coef = {}
        for b in range(5):
            coef[4 * e + b] = STIFF[a, b] / LUMPED[a]
        if a == 0 and e > 0:
            for b in range(5):
                n = 4 * e - 4 + b
                coef[n] = coef.get(n, 0.0) + STIFF[4, b] / LUMPED[0]
        out.append(weighted(layers, {n: c for n, c in coef.items() if n < 4 * elems}))
    return out


def last_partial(layers, elems):
    return weighted(layers, {4 * elems - 4 + b: STIFF[4, b] / LUMPED[0] for b in range(4)})


def element_lines(layers, elems):
    out = []
    for e in range(elems):
        coef = {4 * e + a: WEIGHTS[a] for a in range(5) if 4 * e + a < 4 * elems}
        out.append(weighted(layers, coef))
    out.append(layers[0] * jnp.float32(WEIGHTS[4]))
    return out


def pattern(index, values):
    total = jnp.full(index.shape, values[-1], jnp.float32)
    for a in range(len(values) - 1):
        total = jnp.where(index == a, jnp.float32(values[a]), total)
    return total


def kernel(sizes, elems, *refs):
    (
        adj_hbm, zones_hbm, table, stiff_hbm, zexp_hbm, zred_hbm,
        prior, kgrad,
        adj, zones, stiff_z, zexp, zred,
        scaled, work, diag, lines, face_send, face_recv, z_send, z_recv,
        t_send, t_recv, e_send, e_recv, load_sem, send_sem, recv_sem,
    ) = refs
    ex, ey, ez = elems
    nx, ny, nz = 4 * ex, 4 * ey, 4 * ez
    tiles = nx * ny // 8
    loads = [
        pltpu.make_async_copy(src, dst, load_sem.at[n])
        for n, (src, dst) in enumerate(
            ((zones_hbm, zones), (zexp_hbm, zexp), (adj_hbm, adj), (stiff_hbm, stiff_z), (zred_hbm, zred))
        )
    ]
    for copy in loads:
        copy.start()
    me = tuple(lax.axis_index(a) for a in AXES)
    low = tuple(jnp.minimum(m, 1) for m in me)
    high = tuple(jnp.minimum(s - 1 - m, 1) for m, s in zip(me, sizes))

    def exists(flags, off):
        ok = None
        for f, o in zip(flags, off):
            if o:
                ok = f if ok is None else ok * f
        return ok == 1

    def shifted(off, sign):
        return {a: m + sign * o for a, m, o in zip(AXES, me, off) if o}

    barrier = pltpu.get_barrier_semaphore()
    for off in reversed(OFFSETS):
        for flags, sign in ((high, 1), (low, -1)):
            @pl.when(exists(flags, off))
            def _():
                pl.semaphore_signal(
                    barrier, inc=1, device_id=shifted(off, sign),
                    device_id_type=pl.DeviceIdType.MESH,
                )

    started = []

    def message(src, dst, num, off, sign):
        copy = pltpu.make_async_remote_copy(
            src_ref=src, dst_ref=dst, send_sem=send_sem.at[num], recv_sem=recv_sem.at[num],
            device_id=shifted(off, sign), device_id_type=pl.DeviceIdType.MESH,
        )
        to, come = (high, low) if sign > 0 else (low, high)
        started.append((copy, to, off))

        @pl.when(exists(to, off))
        def _():
            copy.start()

        def arrived():
            @pl.when(exists(come, off))
            def _():
                copy.wait_recv()

        return arrived

    has_low = [f == 1 for f in low]
    has_high = [f == 1 for f in high]
    zero, one = jnp.float32(0.0), jnp.float32(1.0)
    first = [jnp.where(h, one, jnp.float32(2.0)) for h in has_low]
    lane = lax.broadcasted_iota(jnp.int32, (1, nz), 1)
    lane8 = lax.broadcasted_iota(jnp.int32, (8, nz), 1)
    row = lax.broadcasted_iota(jnp.int32, (ny, nz), 0)
    col = lax.broadcasted_iota(jnp.int32, (ny, nz), 1)
    ends = list(STIFF[:4, 4] / LUMPED)
    sends = list(STIFF[4, :4] / LUMPED[0])
    take_first = jnp.where(lane == 0, one, zero)
    take_last = pattern(lane - (nz - 4), ends + [0.0])
    send_last = pattern(lane - (nz - 4), sends + [0.0])

    def xs(ref, i):
        return ref[i * ny : (i + 1) * ny, :]

    def ys(ref, j):
        return ref[pl.ds(j, nx, stride=ny), :]

    def fill_faces(src, phase):
        face_send[phase, 0] = last_partial({i: xs(src, i) for i in range(nx - 4, nx)}, ex)
        face_send[phase, 1] = last_partial({j: ys(src, j) for j in range(ny - 4, ny)}, ey)
        face_send[phase, 2] = ys(src, 0)
        packed = jnp.zeros((8, nz), jnp.float32)
        for v in range(tiles):
            tile = src[8 * v : 8 * v + 8, :]
            total = jnp.sum(tile * send_last, axis=1, keepdims=True)
            packed = jnp.where(lane8 == v, total, packed)
            packed = jnp.where(lane8 == tiles + v, tile[:, 0:1], packed)
        z_send[phase] = packed

    def send_faces(src, phase):
        base = 6 * phase
        return [
            message(z_send.at[phase], z_recv.at[phase, 0], base + 4, (0, 0, 1), 1),
            message(z_send.at[phase], z_recv.at[phase, 1], base + 5, (0, 0, 1), -1),
            message(face_send.at[phase, 1], face_recv.at[phase, 2], base + 2, (0, 1, 0), 1),
            message(face_send.at[phase, 2], face_recv.at[phase, 3], base + 3, (0, 1, 0), -1),
            message(face_send.at[phase, 0], face_recv.at[phase, 0], base, (1, 0, 0), 1),
            message(src.at[0:ny], face_recv.at[phase, 1], base + 1, (1, 0, 0), -1),
        ]

    def own_terms(src):
        along_z = dot(src[...], stiff_z[...]) * jnp.where(lane == 0, first[2], one)
        ylines = line_terms([ys(src, j) for j in range(ny)], ey)
        for j in range(ny):
            work[pl.ds(j, nx, stride=ny), :] = ylines[j] * first[1] if j == 0 else ylines[j]
        xlines = line_terms([xs(src, i) for i in range(nx)], ex)
        for i in range(nx):
            term = xlines[i] * first[0] if i == 0 else xlines[i]
            work[i * ny : (i + 1) * ny, :] += term + along_z[i * ny : (i + 1) * ny, :]

    def halo_terms(phase):
        py = jnp.where(has_low[1], face_recv[phase, 2], zero)
        uy = jnp.where(has_high[1], face_recv[phase, 3], zero)
        work[pl.ds(0, nx, stride=ny), :] += py
        for a in range(4):
            work[pl.ds(ny - 4 + a, nx, stride=ny), :] += uy * jnp.float32(ends[a])
        px = jnp.where(has_low[0], face_recv[phase, 0], zero)
        ux = jnp.where(has_high[0], face_recv[phase, 1], zero)
        zlow = jnp.where(has_low[2], z_recv[phase, 0], zero)
        zhigh = jnp.where(has_high[2], z_recv[phase, 1], zero)

        def layer(i):
            parts = []
            for v in range(i * ny // 8, (i + 1) * ny // 8):
                parts.append(
                    zlow[:, v : v + 1] * take_first
                    + zhigh[:, tiles + v : tiles + v + 1] * take_last
                )
            total = jnp.concatenate(parts, axis=0)
            if i == 0:
                total = total + px
            if i >= nx - 4:
                total = total + ux * jnp.float32(ends[i - nx + 4])
            return total

        return layer

    def kappa_of(values):
        kappa = jnp.zeros(values.shape, jnp.float32)
        for zone in range(table.shape[0]):
            kappa = jnp.where(values == zone, table[zone], kappa)
        return kappa

    block = ex * ey
    loads[0].wait()
    loads[1].wait()
    own_kappa = [kappa_of(zones[e]) for e in range(ex)]
    kappa_sq = jnp.concatenate([k * k for k in own_kappa], axis=0)
    spread_z = dot(kappa_sq, zexp[...])
    t_send[0] = spread_z[:, :nz]
    t_send[1] = spread_z[:, nz:]
    ups = functools.reduce(lambda a, b: a * b, [1 + f for f in high])
    downs = functools.reduce(lambda a, b: a * b, [1 + f for f in low])
    pl.semaphore_wait(barrier, ups + downs - 2)
    t_got = []
    for n, off in reversed(list(enumerate(OFFSETS))):
        t_got.append(message(t_send.at[off[2]], t_recv.at[n], 12 + n, off, 1))
    loads[2].wait()
    fill_faces(adj, 0)
    got = send_faces(adj, 0)

    loads[3].wait()
    own_terms(adj)
    at_y, at_z = row == 0, col == 0
    doubled = jnp.where(at_y, first[1], one) * jnp.where(at_z, first[2], one)
    end_y = jnp.where(at_y, jnp.where(has_low[1], jnp.float32(END_DIAG), zero), zero)
    end_yz = end_y + jnp.where(at_z, jnp.where(has_low[2], jnp.float32(END_DIAG), zero), zero)
    end_x = jnp.where(has_low[0], jnp.float32(END_DIAG), zero)
    mass_yz = pattern(lax.rem(row, 4), list(LUMPED)) * pattern(lax.rem(col, 4), list(LUMPED))
    mass_yz = mass_yz * jnp.float32(0.001) / doubled
    y_coef = []
    for f in range(-1, ey):
        local = row - 4 * f
        y_coef.append(pattern(local, list(WN) + [WN0, 0.0]) * doubled)

    for w in got:
        w()
    layer = halo_terms(0)
    for i in range(nx):
        work[i * ny : (i + 1) * ny, :] += layer(i)

    for w in t_got:
        w()

    def spread_at(sx, sy):
        total = None
        for sz in range(2):
            off = (sx, sy, sz)
            if off == (0, 0, 0):
                part = t_send[0]
            else:
                part = jnp.where(exists(low, off), t_recv[OFFSETS.index(off)], zero)
            total = part if total is None else total + part
        return total

    slots = {(sx, sy): spread_at(sx, sy) for sx in range(2) for sy in range(2)}
    columns = []
    for e in range(-1, ex):
        total = None
        for f in range(-1, ey):
            source = slots[(int(e < 0), int(f < 0))]
            r = (e % ex) * ey + f % ey
            term = source[r : r + 1, :] * y_coef[f + 1]
            total = term if total is None else total + term
        columns.append(total)
    for i in range(nx):
        e, a = divmod(i, 4)
        if a == 0:
            mass = (columns[e + 1] + columns[e]) * jnp.float32(WN0)
        else:
            mass = columns[e + 1] * jnp.float32(WN[a])
        value = mass * first[0] + (end_yz + end_x) if i == 0 else mass + end_yz
        rows = slice(i * ny, (i + 1) * ny)
        diag[rows, :] = value
        scaled[rows, :] = work[rows, :] + value * adj[rows, :]

    ysums = element_lines([ys(adj, j) * ys(scaled, j) for j in range(ny)], ey)
    for f in range(8):
        lines[f * nx : (f + 1) * nx, :] = ysums[f] if f <= ey else jnp.zeros((nx, nz), jnp.float32)
    xsums = element_lines([lines[pl.ds(i, 8, stride=nx), :] for i in range(nx)], ex)
    xsums = jnp.concatenate(xsums, axis=0)
    loads[4].wait()
    for sz in range(2):
        e_send[sz] = dot(xsums, zred[sz])
    e_got = []
    for n, off in reversed(list(enumerate(OFFSETS))):
        rows = pl.ds(8 * ex, 8) if off[0] else pl.ds(0, 8 * ex)
        e_got.append(message(e_send.at[off[2], rows], e_recv.at[n, rows], 19 + n, off, -1))

    fill_faces(scaled, 1)
    got = send_faces(scaled, 1)

    own_terms(scaled)
    work[...] += diag[...] * scaled[...]
    for w in got:
        w()
    layer = halo_terms(1)
    for i in range(nx):
        rows = slice(i * ny, (i + 1) * ny)
        factor = mass_yz * jnp.float32(LUMPED[i % 4])
        if i == 0:
            factor = factor / first[0]
        prior[rows, :] = (work[rows, :] + layer(i)) * factor

    for copy, to, off in started:
        @pl.when(exists(to, off))
        def _():
            copy.wait_send()

    for w in e_got:
        w()
    row8 = lax.broadcasted_iota(jnp.int32, (8, ez), 0)
    for e in range(ex):
        total = e_send[0, 8 * e : 8 * e + 8]
        above = jnp.zeros((8, ez), jnp.float32)
        for n, off in enumerate(OFFSETS):
            if off[0] and e < ex - 1:
                continue
            start = 8 * ex if off[0] else 8 * e
            part = jnp.where(exists(high, off), e_recv[n, start : start + 8], zero)
            if off[1]:
                above = above + part
            else:
                total = total + part
        total = total + jnp.where(row8 == ey - 1, pltpu.roll(above, 7, 0), zero)
        kgrad[e] = total[:ey] * (own_kappa[e] * jnp.float32(0.002))


def finish(prior, kgrad, prior_out, kgrad_out):
    prior_out[...] = prior[...]
    kgrad_out[...] = kgrad[...]


def on_device(sizes, adjoint, element_zone_index, kappa_table):
    nx, ny, nz = adjoint.shape
    elems = ex, ey, ez = element_zone_index.shape
    consts = [jnp.asarray(c) for c in constants(ez)]
    f32 = jnp.float32
    vmem = pl.BlockSpec(memory_space=pltpu.VMEM)
    hbm = pl.BlockSpec(memory_space=pltpu.HBM)
    prior, kgrad = pl.pallas_call(
        functools.partial(kernel, sizes, elems),
        out_shape=(
            jax.ShapeDtypeStruct((nx * ny, nz), f32),
            jax.ShapeDtypeStruct((ex, ey, ez), f32),
        ),
        in_specs=[hbm, hbm, pl.BlockSpec(memory_space=pltpu.SMEM)] + [hbm] * len(consts),
        out_specs=(vmem, vmem),
        scratch_shapes=[
            pltpu.VMEM((nx * ny, nz), f32),
            pltpu.VMEM((ex, ey, ez), jnp.int32),
            pltpu.VMEM(consts[0].shape, f32),
            pltpu.VMEM(consts[1].shape, f32),
            pltpu.VMEM(consts[2].shape, f32),
            pltpu.VMEM((nx * ny, nz), f32),
            pltpu.VMEM((nx * ny, nz), f32),
            pltpu.VMEM((nx * ny, nz), f32),
            pltpu.VMEM((8 * nx, nz), f32),
            pltpu.VMEM((2, 3, ny, nz), f32),
            pltpu.VMEM((2, 4, ny, nz), f32),
            pltpu.VMEM((2, 8, nz), f32),
            pltpu.VMEM((2, 2, 8, nz), f32),
            pltpu.VMEM((2, ex * ey, nz), f32),
            pltpu.VMEM((7, ex * ey, nz), f32),
            pltpu.VMEM((2, 8 * ex + 8, ez), f32),
            pltpu.VMEM((7, 8 * ex + 8, ez), f32),
            pltpu.SemaphoreType.DMA((5,)),
            pltpu.SemaphoreType.DMA((26,)),
            pltpu.SemaphoreType.DMA((26,)),
        ],
        compiler_params=pltpu.CompilerParams(
            collective_id=0, has_side_effects=True
        ),
        name="bilaplacian",
    )(adjoint.reshape(nx * ny, nz), element_zone_index, kappa_table, *consts)
    prior, kgrad = pl.pallas_call(
        finish,
        out_shape=(
            jax.ShapeDtypeStruct((nx * ny, nz), f32),
            jax.ShapeDtypeStruct((ex, ey, ez), f32),
        ),
        in_specs=[vmem, vmem],
        out_specs=(vmem, vmem),
        name="finish",
    )(prior, kgrad)
    return prior.reshape(nx, ny, nz), kgrad


def solution(mesh):
    sizes = tuple(mesh.shape[a] for a in AXES)
    return jax.shard_map(
        functools.partial(on_device, sizes), mesh=mesh,
        in_specs=(P("gx", "gy", "gz"), P("gx", "gy", "gz"), P()),
        out_specs=(P("gx", "gy", "gz"), P("gx", "gy", "gz")), check_vma=False,
    )
```

profile of v0, /device:TPU:0, one launch (start us, length us, event | category | flops | bytes accessed | tf_op | source)
XLA Modules:
  0.0 15.7 jit_solution(15698634577783811404)
XLA Ops:
  0.6 13.5 %bilaplacian.1 = (f32[256,128]{1,0:T(8,128)}, f32[4,4,32]{2,1,0:T(4,128)}) custom-call(f32[256,128]{1,0:T(8,128)} %bitcast.2, s32[4,4,32]{2,1,0:T(4,128)} %refs_1_.1, f32[8]{0:T(128)} %refs_2_.1, f32[128,128]{1,0:T(8,128)} %constant.6.clone.refs_3_, f32[32,256]{1,0:T(8,128)} %constant.7.clone.refs_4_, f32[2,128,32]{2,1,0:T(8,128)} %constant.8.clone.refs_5_), custom_call_target="tpu_custom_call" | custom-call | tf_op jit(solution)/shard_map/bilaplacian/pallas_call | solution.py:393
  14.1 1.6 %finish.1 = (f32[256,128]{1,0:T(8,128)}, f32[4,4,32]{2,1,0:T(4,128)}) custom-call(f32[256,128]{1,0:T(8,128)} %get-tuple-element.6.prior, f32[4,4,32]{2,1,0:T(4,128)} %get-tuple-element.7.kgrad), custom_call_target="tpu_custom_call" | custom-call | tf_op jit(solution)/shard_map/finish/pallas_call | solution.py:428
where the time goes:
time: 15.9 us; the launch traced here: 15.7 us
  Pallas kernels  15.1 us (95%)
  between operations  0.64 us (4%)
    pallas_call x1, Pallas kernels, on_device(): pl.pallas_call(functools.partial(kernel, sizes, elems), out_shape=(jax.Sh...  13.5 us
    pallas_call x1, Pallas kernels, on_device(): pl.pallas_call(finish, out_shape=(jax.ShapeDtypeStruct((nx * ny, nz), f32...  1.57 us

commit v1 on v0

--- a/solution.py
+++ b/solution.py
@@ -105,9 +105,9 @@
 
 def kernel(sizes, elems, *refs):
     (
-        adj_hbm, zones_hbm, table, stiff_hbm, zexp_hbm, zred_hbm,
+        adj_hbm, zones_hbm, table_hbm, stiff_hbm, zexp_hbm, zred_hbm,
         prior, kgrad,
-        adj, zones, stiff_z, zexp, zred,
+        adj, zones, table, stiff_z, zexp, zred,
         scaled, work, diag, lines, face_send, face_recv, z_send, z_recv,
         t_send, t_recv, e_send, e_recv, load_sem, send_sem, recv_sem,
     ) = refs
@@ -117,7 +117,7 @@
     loads = [
         pltpu.make_async_copy(src, dst, load_sem.at[n])
         for n, (src, dst) in enumerate(
-            ((zones_hbm, zones), (zexp_hbm, zexp), (adj_hbm, adj), (stiff_hbm, stiff_z), (zred_hbm, zred))
+            ((zones_hbm, zones), (zexp_hbm, zexp), (adj_hbm, adj), (stiff_hbm, stiff_z), (zred_hbm, zred), (table_hbm, table))
         )
     ]
     for copy in loads:
@@ -254,6 +254,7 @@
         return kappa
 
     block = ex * ey
+    loads[5].wait()
     loads[0].wait()
     loads[1].wait()
     own_kappa = [kappa_of(zones[e]) for e in range(ex)]
@@ -378,9 +379,15 @@
         kgrad[e] = total[:ey] * (own_kappa[e] * jnp.float32(0.002))
 
 
-def finish(prior, kgrad, prior_out, kgrad_out):
-    prior_out[...] = prior[...]
-    kgrad_out[...] = kgrad[...]
+def finish(prior, kgrad, prior_out, kgrad_out, sem):
+    copies = [
+        pltpu.make_async_copy(src, dst, sem.at[n])
+        for n, (src, dst) in enumerate(((prior, prior_out), (kgrad, kgrad_out)))
+    ]
+    for copy in copies:
+        copy.start()
+    for copy in copies:
+        copy.wait()
 
 
 def on_device(sizes, adjoint, element_zone_index, kappa_table):
@@ -392,15 +399,13 @@
     hbm = pl.BlockSpec(memory_space=pltpu.HBM)
     prior, kgrad = pl.pallas_call(
         functools.partial(kernel, sizes, elems),
-        out_shape=(
-            jax.ShapeDtypeStruct((nx * ny, nz), f32),
-            jax.ShapeDtypeStruct((ex, ey, ez), f32),
-        ),
-        in_specs=[hbm, hbm, pl.BlockSpec(memory_space=pltpu.SMEM)] + [hbm] * len(consts),
+        out_shape=(pltpu.VMEM((nx * ny, nz), f32), pltpu.VMEM((ex, ey, ez), f32)),
+        in_specs=[hbm] * (3 + len(consts)),
         out_specs=(vmem, vmem),
         scratch_shapes=[
             pltpu.VMEM((nx * ny, nz), f32),
             pltpu.VMEM((ex, ey, ez), jnp.int32),
+            pltpu.SMEM(kappa_table.shape, f32),
             pltpu.VMEM(consts[0].shape, f32),
             pltpu.VMEM(consts[1].shape, f32),
             pltpu.VMEM(consts[2].shape, f32),
@@ -416,7 +421,7 @@
             pltpu.VMEM((7, ex * ey, nz), f32),
             pltpu.VMEM((2, 8 * ex + 8, ez), f32),
             pltpu.VMEM((7, 8 * ex + 8, ez), f32),
-            pltpu.SemaphoreType.DMA((5,)),
+            pltpu.SemaphoreType.DMA((6,)),
             pltpu.SemaphoreType.DMA((26,)),
             pltpu.SemaphoreType.DMA((26,)),
         ],
@@ -432,9 +437,10 @@
             jax.ShapeDtypeStruct((ex, ey, ez), f32),
         ),
         in_specs=[vmem, vmem],
-        out_specs=(vmem, vmem),
+        out_specs=(hbm, hbm),
+        scratch_shapes=[pltpu.SemaphoreType.DMA((2,))],
         name="finish",
-    )(prior, kgrad)
+    )(*(pltpu.with_memory_space_constraint(r, pltpu.VMEM) for r in (prior, kgrad)))
     return prior.reshape(nx, ny, nz), kgrad
 
 

time: 15.9 us -> 13.7 us (0.86)
  Pallas kernels: 15.1 us -> 12.9 us
    pallas_call x1, Pallas kernels: 13.5 us -> 12.2 us  [on_device(): pl.pallas_call(functools.partial(kernel, sizes, elems), out_shape=(pltpu....]
    pallas_call x1, Pallas kernels: 1.57 us -> 0.68 us  [on_device(): pl.pallas_call(finish, out_shape=(jax.ShapeDtypeStruct((nx * ny, nz), f32...]
where the time goes in v1:
time: 13.7 us; the launch traced here: 13.5 us
  Pallas kernels  12.9 us (94%)
  between operations  0.64 us (5%)
    pallas_call x1, Pallas kernels, on_device(): pl.pallas_call(functools.partial(kernel, sizes, elems), out_shape=(pltpu....  12.2 us
    pallas_call x1, Pallas kernels, on_device(): pl.pallas_call(finish, out_shape=(jax.ShapeDtypeStruct((nx * ny, nz), f32...  0.68 us

profile of v1, /device:TPU:0, one launch (start us, length us, event | category | flops | bytes accessed | tf_op | source)
XLA Modules:
  0.0 13.5 jit_solution(17249426823040711200)
XLA Ops:
  0.6 12.2 %bilaplacian.1 = (f32[256,128]{1,0:T(8,128)S(1)}, f32[4,4,32]{2,1,0:T(4,128)S(1)}) custom-call(f32[256,128]{1,0:T(8,128)} %bitcast.2, s32[4,4,32]{2,1,0:T(4,128)} %refs_1_.1, f32[8]{0:T(128)} %refs_2_.1, f32[128,128]{1,0:T(8,128)} %constant.6.clone.refs_3_, f32[32,256]{1,0:T(8,128)} %constant.7.clone.refs_4_, f32[2,128,32]{2,1,0:T(8,128)} %constant.8.clone.refs_5_), custom_call_target="tpu_custom_call" | custom-call | tf_op jit(solution)/shard_map/bilaplacian/pallas_call | solution.py:400
  12.8 0.7 %finish.1 = (f32[256,128]{1,0:T(8,128)}, f32[4,4,32]{2,1,0:T(4,128)}) custom-call(f32[256,128]{1,0:T(8,128)S(1)} %get-tuple-element.6.prior, f32[4,4,32]{2,1,0:T(4,128)S(1)} %get-tuple-element.7.kgrad), custom_call_target="tpu_custom_call" | custom-call | tf_op jit(solution)/shard_map/finish/pallas_call | solution.py:433

commit v2 on v1

--- a/solution.py
+++ b/solution.py
@@ -40,19 +40,17 @@
 def constants(ez):
     nodes = 4 * ez
     stiff_z = np.zeros((nodes, nodes))
-    zexp = np.zeros((ez, 2 * nodes))
-    zred = np.zeros((2, nodes, ez))
+    zexp = np.zeros((ez, nodes))
+    zred = np.zeros((nodes, ez))
     for e in range(ez):
         for a in range(5):
             k = 4 * e + a
             if k < nodes:
                 zexp[e, k] += WEIGHTS[a] / LUMPED[a % 4]
-                zred[0, k, e] += WEIGHTS[a]
+                zred[k, e] += WEIGHTS[a]
                 for b in range(5):
                     if 4 * e + b < nodes:
                         stiff_z[4 * e + b, k] += STIFF[a, b] / LUMPED[a % 4]
-    zexp[ez - 1, nodes] = WN0
-    zred[1, 0, ez - 1] = WEIGHTS[4]
     return tuple(np.asarray(c, np.float32) for c in (stiff_z, zexp, zred))
 
 
@@ -109,7 +107,9 @@
         prior, kgrad,
         adj, zones, table, stiff_z, zexp, zred,
         scaled, work, diag, lines, face_send, face_recv, z_send, z_recv,
-        t_send, t_recv, e_send, e_recv, load_sem, send_sem, recv_sem,
+        tx_send, ty_send, txy_send, tx_recv, ty_recv, txy_recv,
+        e_own, ey_send, exy_send, ez_send, ezy_send,
+        ex_recv, ey_recv, exy_recv, ez_recv, ezy_recv, load_sem, send_sem, recv_sem,
     ) = refs
     ex, ey, ez = elems
     nx, ny, nz = 4 * ex, 4 * ey, 4 * ez
@@ -120,8 +120,8 @@
             ((zones_hbm, zones), (zexp_hbm, zexp), (adj_hbm, adj), (stiff_hbm, stiff_z), (zred_hbm, zred), (table_hbm, table))
         )
     ]
-    for copy in loads:
-        copy.start()
+    for n in (2, 0, 5, 1, 3, 4):
+        loads[n].start()
     me = tuple(lax.axis_index(a) for a in AXES)
     low = tuple(jnp.minimum(m, 1) for m in me)
     high = tuple(jnp.minimum(s - 1 - m, 1) for m, s in zip(me, sizes))
@@ -187,7 +187,7 @@
     def ys(ref, j):
         return ref[pl.ds(j, nx, stride=ny), :]
 
-    def fill_faces(src, phase):
+    def fill_faces(src, phase, extra=()):
         face_send[phase, 0] = last_partial({i: xs(src, i) for i in range(nx - 4, nx)}, ex)
         face_send[phase, 1] = last_partial({j: ys(src, j) for j in range(ny - 4, ny)}, ey)
         face_send[phase, 2] = ys(src, 0)
@@ -197,6 +197,8 @@
             total = jnp.sum(tile * send_last, axis=1, keepdims=True)
             packed = jnp.where(lane8 == v, total, packed)
             packed = jnp.where(lane8 == tiles + v, tile[:, 0:1], packed)
+        for n, column in enumerate(extra):
+            packed = jnp.where(lane8 == 2 * tiles + n, column, packed)
         z_send[phase] = packed
 
     def send_faces(src, phase):
@@ -260,16 +262,23 @@
     own_kappa = [kappa_of(zones[e]) for e in range(ex)]
     kappa_sq = jnp.concatenate([k * k for k in own_kappa], axis=0)
     spread_z = dot(kappa_sq, zexp[...])
-    t_send[0] = spread_z[:, :nz]
-    t_send[1] = spread_z[:, nz:]
+    end_z = kappa_sq[:, ez - 1 :] * jnp.float32(WN0)
+    for sz, rows in enumerate((spread_z, end_z * take_first)):
+        tx_send[sz] = rows[block - ey :]
+        for e in range(ex):
+            ty_send[sz, e : e + 1] = rows[(e + 1) * ey - 1 : (e + 1) * ey]
+        txy_send[sz] = rows[block - 1 :]
+    loads[2].wait()
+    fill_faces(adj, 0, [end_z[8 * n : 8 * n + 8] for n in range(block // 8)])
     ups = functools.reduce(lambda a, b: a * b, [1 + f for f in high])
     downs = functools.reduce(lambda a, b: a * b, [1 + f for f in low])
     pl.semaphore_wait(barrier, ups + downs - 2)
     t_got = []
     for n, off in reversed(list(enumerate(OFFSETS))):
-        t_got.append(message(t_send.at[off[2]], t_recv.at[n], 12 + n, off, 1))
-    loads[2].wait()
-    fill_faces(adj, 0)
+        if off == (0, 0, 1):
+            continue
+        send, recv = {(1, 0): (tx_send, tx_recv), (0, 1): (ty_send, ty_recv), (1, 1): (txy_send, txy_recv)}[off[:2]]
+        t_got.append(message(send.at[off[2]], recv.at[off[2]], 12 + n, off, 1))
     got = send_faces(adj, 0)
 
     loads[3].wait()
@@ -295,25 +304,27 @@
     for w in t_got:
         w()
 
-    def spread_at(sx, sy):
-        total = None
-        for sz in range(2):
-            off = (sx, sy, sz)
-            if off == (0, 0, 0):
-                part = t_send[0]
-            else:
-                part = jnp.where(exists(low, off), t_recv[OFFSETS.index(off)], zero)
-            total = part if total is None else total + part
-        return total
-
-    slots = {(sx, sy): spread_at(sx, sy) for sx in range(2) for sy in range(2)}
+    def low_sum(recv, sx, sy):
+        parts = [jnp.where(exists(low, (sx, sy, sz)), recv[sz], zero) for sz in range(2)]
+        return parts[0] + parts[1]
+
+    low_x, low_y, low_xy = low_sum(tx_recv, 1, 0), low_sum(ty_recv, 0, 1), low_sum(txy_recv, 1, 1)
+    zlow = jnp.where(has_low[2], z_recv[0, 0], zero)
+    low_z = [zlow[:, 2 * tiles + n : 2 * tiles + n + 1] for n in range(block // 8)]
+    own = spread_z + jnp.concatenate(low_z, axis=0) * take_first
+
+    def spread_row(e, f):
+        if e >= 0 and f >= 0:
+            return own[e * ey + f : e * ey + f + 1]
+        if f >= 0:
+            return low_x[f : f + 1]
+        return low_y[e : e + 1] if e >= 0 else low_xy
+
     columns = []
     for e in range(-1, ex):
         total = None
         for f in range(-1, ey):
-            source = slots[(int(e < 0), int(f < 0))]
-            r = (e % ex) * ey + f % ey
-            term = source[r : r + 1, :] * y_coef[f + 1]
+            term = spread_row(e, f) * y_coef[f + 1]
             total = term if total is None else total + term
         columns.append(total)
     for i in range(nx):
@@ -331,17 +342,32 @@
     for f in range(8):
         lines[f * nx : (f + 1) * nx, :] = ysums[f] if f <= ey else jnp.zeros((nx, nz), jnp.float32)
     xsums = element_lines([lines[pl.ds(i, 8, stride=nx), :] for i in range(nx)], ex)
-    xsums = jnp.concatenate(xsums, axis=0)
-    loads[4].wait()
-    for sz in range(2):
-        e_send[sz] = dot(xsums, zred[sz])
+    packed = jnp.zeros((8, nz), jnp.float32)
+    for e in range(ex + 1):
+        packed = jnp.where(lane8 == e, xsums[e][:, 0:1] * jnp.float32(WEIGHTS[4]), packed)
+    ez_send[...] = packed
+    ezy_send[...] = packed[ey : ey + 1]
     e_got = []
-    for n, off in reversed(list(enumerate(OFFSETS))):
-        rows = pl.ds(8 * ex, 8) if off[0] else pl.ds(0, 8 * ex)
-        e_got.append(message(e_send.at[off[2], rows], e_recv.at[n, rows], 19 + n, off, -1))
-
+
+    def send_sums(off, src, dst):
+        e_got.append(message(src, dst, 19 + OFFSETS.index(off), off, -1))
+
+    send_sums((1, 1, 1), ezy_send, ezy_recv.at[1])
+    send_sums((0, 1, 1), ezy_send, ezy_recv.at[0])
+    send_sums((1, 0, 1), ez_send, ez_recv.at[1])
+    send_sums((0, 0, 1), ez_send, ez_recv.at[0])
     fill_faces(scaled, 1)
     got = send_faces(scaled, 1)
+
+    loads[4].wait()
+    zsums = dot(jnp.concatenate(xsums, axis=0), zred[...])
+    e_own[...] = zsums
+    for e in range(ex):
+        ey_send[e : e + 1] = zsums[8 * e + ey : 8 * e + ey + 1]
+    exy_send[...] = zsums[8 * ex + ey : 8 * ex + ey + 1]
+    send_sums((1, 1, 0), exy_send, exy_recv)
+    send_sums((0, 1, 0), ey_send, ey_recv)
+    send_sums((1, 0, 0), e_own.at[8 * ex : 8 * ex + 8], ex_recv)
 
     own_terms(scaled)
     work[...] += diag[...] * scaled[...]
@@ -363,19 +389,23 @@
     for w in e_got:
         w()
     row8 = lax.broadcasted_iota(jnp.int32, (8, ez), 0)
+    at_end = lax.broadcasted_iota(jnp.int32, (1, ez), 1) == ez - 1
+
+    def from_high(value, off):
+        return jnp.where(exists(high, off), value, zero)
+
     for e in range(ex):
-        total = e_send[0, 8 * e : 8 * e + 8]
-        above = jnp.zeros((8, ez), jnp.float32)
-        for n, off in enumerate(OFFSETS):
-            if off[0] and e < ex - 1:
-                continue
-            start = 8 * ex if off[0] else 8 * e
-            part = jnp.where(exists(high, off), e_recv[n, start : start + 8], zero)
-            if off[1]:
-                above = above + part
-            else:
-                total = total + part
-        total = total + jnp.where(row8 == ey - 1, pltpu.roll(above, 7, 0), zero)
+        total = e_own[8 * e : 8 * e + 8]
+        side = from_high(ez_recv[0][:, e : e + 1], (0, 0, 1))
+        corner = from_high(ezy_recv[0][:, e : e + 1], (0, 1, 1))
+        above = from_high(ey_recv[e : e + 1], (0, 1, 0))
+        if e == ex - 1:
+            total = total + from_high(ex_recv[...], (1, 0, 0))
+            side = side + from_high(ez_recv[1][:, ex : ex + 1], (1, 0, 1))
+            corner = corner + from_high(ezy_recv[1][:, ex : ex + 1], (1, 1, 1))
+            above = above + from_high(exy_recv[...], (1, 1, 0))
+        above = above + jnp.where(at_end, corner, zero)
+        total = total + jnp.where(at_end, side, zero) + jnp.where(row8 == ey - 1, above, zero)
         kgrad[e] = total[:ey] * (own_kappa[e] * jnp.float32(0.002))
 
 
@@ -417,10 +447,22 @@
             pltpu.VMEM((2, 4, ny, nz), f32),
             pltpu.VMEM((2, 8, nz), f32),
             pltpu.VMEM((2, 2, 8, nz), f32),
-            pltpu.VMEM((2, ex * ey, nz), f32),
-            pltpu.VMEM((7, ex * ey, nz), f32),
-            pltpu.VMEM((2, 8 * ex + 8, ez), f32),
-            pltpu.VMEM((7, 8 * ex + 8, ez), f32),
+            pltpu.VMEM((2, ey, nz), f32),
+            pltpu.VMEM((2, ex, nz), f32),
+            pltpu.VMEM((2, 1, nz), f32),
+            pltpu.VMEM((2, ey, nz), f32),
+            pltpu.VMEM((2, ex, nz), f32),
+            pltpu.VMEM((2, 1, nz), f32),
+            pltpu.VMEM((8 * ex + 8, ez), f32),
+            pltpu.VMEM((ex, ez), f32),
+            pltpu.VMEM((1, ez), f32),
+            pltpu.VMEM((8, nz), f32),
+            pltpu.VMEM((1, nz), f32),
+            pltpu.VMEM((8, ez), f32),
+            pltpu.VMEM((ex, ez), f32),
+            pltpu.VMEM((1, ez), f32),
+            pltpu.VMEM((2, 8, nz), f32),
+            pltpu.VMEM((2, 1, nz), f32),
             pltpu.SemaphoreType.DMA((6,)),
             pltpu.SemaphoreType.DMA((26,)),
             pltpu.SemaphoreType.DMA((26,)),

time: 13.7 us -> 13.4 us (0.978)
  Pallas kernels: 12.9 us -> 12.6 us
    pallas_call x1, Pallas kernels: 12.2 us -> 12 us  [on_device(): pl.pallas_call(functools.partial(kernel, sizes, elems), out_shape=(pltpu....]
where the time goes in v2:
time: 13.4 us; the launch traced here: 13.3 us
  Pallas kernels  12.6 us (94%)
  between operations  0.64 us (5%)
    pallas_call x1, Pallas kernels, on_device(): pl.pallas_call(functools.partial(kernel, sizes, elems), out_shape=(pltpu....  12 us
    pallas_call x1, Pallas kernels, on_device(): pl.pallas_call(finish, out_shape=(jax.ShapeDtypeStruct((nx * ny, nz), f32...  0.68 us

profile of v2, /device:TPU:0, one launch (start us, length us, event | category | flops | bytes accessed | tf_op | source)
XLA Modules:
  0.0 13.3 jit_solution(15783837258929500783)
XLA Ops:
  0.6 12.0 %bilaplacian.1 = (f32[256,128]{1,0:T(8,128)S(1)}, f32[4,4,32]{2,1,0:T(4,128)S(1)}) custom-call(f32[256,128]{1,0:T(8,128)} %bitcast.2, s32[4,4,32]{2,1,0:T(4,128)} %refs_1_.1, f32[8]{0:T(128)} %refs_2_.1, f32[128,128]{1,0:T(8,128)} %constant.6.clone.refs_3_, f32[32,128]{1,0:T(8,128)} %constant.7.clone.refs_4_, f32[128,32]{1,0:T(8,128)} %constant.8.clone.refs_5_), custom_call_target="tpu_custom_call" | custom-call | tf_op jit(solution)/shard_map/bilaplacian/pallas_call | solution.py:430
  12.6 0.7 %finish.1 = (f32[256,128]{1,0:T(8,128)}, f32[4,4,32]{2,1,0:T(4,128)}) custom-call(f32[256,128]{1,0:T(8,128)S(1)} %get-tuple-element.6.prior, f32[4,4,32]{2,1,0:T(4,128)S(1)} %get-tuple-element.7.kgrad), custom_call_target="tpu_custom_call" | custom-call | tf_op jit(solution)/shard_map/finish/pallas_call | solution.py:475
